TPU v7x, 128 devices: a whole 4x4x4 slice. The times are simulated.
128 devices in a mesh: row: 8 (over z, core), col: 16 (over y, x).
Axes of the slice: x: 4, y: 4, z: 4, core: 2. Of those that a mesh axis runs over, the one named last changes fastest.
Arguments:
- symmetric: float32 [16384, 16384], P('row', 'col'), may hold values from -8 to 8, as said below
- reflectors: float32 [4, 64, 16384], P(None, None, ('row', 'col')), may hold values from -0.125 to 0.125
- tri_factor: float32 [4, 64, 64], replicated, may hold values from -0.4 to 1.5, as said below
Outputs:
- updated: float32 [16384, 16384], P('row', 'col')
Inputs may be any that keep to these rules, and one draw needn't show every extreme that they name: symmetric is a symmetric matrix. Each tri_factor[p] is upper triangular.
All inputs are finite; a program needn't handle non-finite values.
Results may differ from a plain program's by a relative error of at most 0.00029.
Values sent between devices are 32-bit elements; how exact they have to be, the bound alone decides.
A program may use at most 64 MiB of HBM per device.

v0:
```python
import jax
import jax.numpy as jnp
from jax import lax
from jax.sharding import PartitionSpec as P


def broadcast(value, axis, source):
    kept = jnp.where(lax.axis_index(axis) == source, value, 0).astype(value.dtype)
    return lax.psum(kept, axis)


def shards(symmetric, reflectors, tri_factor):
    highest = lax.Precision.HIGHEST
    cols_here = symmetric.shape[1]
    row_count = lax.axis_size("row")
    col_count = lax.axis_size("col")
    col_index = lax.axis_index("col")
    owner = col_index * row_count // col_count
    offset = col_index % (col_count // row_count) * cols_here
    matrix = symmetric
    for panel in range(reflectors.shape[0]):
        piece = reflectors[panel]
        factor = tri_factor[panel]
        reflect_rows = lax.all_gather(piece, "col", axis=1, tiled=True)
        reflect_cols = broadcast(
            lax.dynamic_slice_in_dim(reflect_rows, offset, cols_here, 1), "row", owner
        )
        partial_value = lax.dot_general(
            reflect_cols,
            matrix,
            (((1,), (1,)), ((), ())),
            precision=highest,
            preferred_element_type=jnp.float32,
        )
        product_rows = lax.psum(partial_value, "col")
        image_rows = jnp.dot(
            factor.T, product_rows, precision=highest, preferred_element_type=jnp.float32
        )
        local_inner = lax.dot_general(
            reflect_rows,
            image_rows,
            (((1,), (1,)), ((), ())),
            precision=highest,
            preferred_element_type=jnp.float32,
        )
        inner = lax.psum(local_inner, "row")
        coupling = jnp.dot(factor.T, inner, precision=highest, preferred_element_type=jnp.float32)
        update_rows = image_rows - 0.5 * jnp.dot(
            coupling.T, reflect_rows, precision=highest, preferred_element_type=jnp.float32
        )
        update_cols = broadcast(
            lax.dynamic_slice_in_dim(update_rows, offset, cols_here, 1), "row", owner
        )
        left_block = jnp.concatenate([reflect_rows, update_rows], axis=0)
        right_block = jnp.concatenate([update_cols, reflect_cols], axis=0)
        matrix = matrix - lax.dot_general(
            left_block,
            right_block,
            (((0,), (0,)), ((), ())),
            precision=highest,
            preferred_element_type=jnp.float32,
        )
    return matrix


def solution(mesh):
    placed = (P("row", "col"), P(None, None, ("row", "col")), P())
    return jax.shard_map(
        shards, mesh=mesh, in_specs=placed, out_specs=P("row", "col"), check_vma=False
    )
```

profile of v0, /device:TPU:0, one launch (start us, length us, event | category | flops | bytes accessed | tf_op | source)
XLA Modules:
  0.0 878.7 jit_solution(7771888216284126579)
XLA Ops:
  7.4 25.2 %all-gather = f32[1,64,2048]{2,1,0:T(8,128)S(1)} all-gather(f32[1,64,128]{2,1,0:T(8,128)S(1)} %get-tuple-element.13), channel_id=2, replica_groups=mesh['row'=8,'col'=16] {'col'}, dimensions={2}, use_global_device_ids=true | all-gather | bytes 557056 | tf_op jit(solution)/shard_map/all_gather | solution.py:24
  33.4 60.0 %all-reduce.13.cloned.1.call-done = f32[64,1024]{1,0:T(8,128)} async-done(((f32[64,1024]{1,0:T(8,128)}), f32[64,1024]{1,0:T(8,128)}) %all-reduce.13.cloned.1.call-update) | async-done | bytes 262160 | tf_op jit(solution)/shard_map/psum | solution.py:9
  93.4 12.3 %fusion.65 = f32[64,2048]{1,0:T(8,128)} fusion(f32[64,1024]{1,0:T(8,128)} %all-reduce.13.cloned.1.call-done, f32[2048,1024]{1,0:T(8,128)} %param.3), kind=kOutput, calls=%fused_computation.85 | convolution fusion | flops 1610612736 | bytes 9175040 | tf_op jit(solution)/shard_map/dot_general | solution.py:28
  105.7 25.3 %all-gather.1 = f32[1,64,2048]{2,1,0:T(8,128)S(1)} all-gather(f32[1,64,128]{2,1,0:T(8,128)S(1)} %get-tuple-element.12), channel_id=3, replica_groups=mesh['row'=8,'col'=16] {'col'}, dimensions={2}, use_global_device_ids=true | all-gather | bytes 557056 | tf_op jit(solution)/shard_map/all_gather | solution.py:24
  131.7 58.1 %all-reduce.15.cloned.1.call-done = f32[64,2048]{1,0:T(8,128)} async-done(((f32[64,2048]{1,0:T(8,128)}), f32[64,2048]{1,0:T(8,128)}) %all-reduce.15.cloned.1.call-update) | async-done | bytes 524304 | tf_op jit(solution)/shard_map/psum | solution.py:35
  192.1 24.4 %psum.114 = f32[64,64]{0,1:T(8,128)S(1)} all-reduce(f32[64,64]{0,1:T(8,128)S(1)} %convolution_bitcast_fusion.3), channel_id=1, replica_groups=mesh['row'=8,'col'=16] {'row'}, use_global_device_ids=true, to_apply=%region_2.3 | all-reduce | flops 4096 | bytes 32768 | tf_op jit(solution)/shard_map/psum | solution.py:46
  218.3 57.3 %all-reduce.29.cloned.1.call-done = (f32[64,1024]{1,0:T(8,128)}, f32[64,1024]{1,0:T(8,128)}) async-done(((f32[64,1024]{1,0:T(8,128)}, f32[64,1024]{1,0:T(8,128)}), (f32[64,1024]{1,0:T(8,128)}, f32[64,1024]{1,0:T(8,128)})) %all-reduce.29.cloned.1.call-update) | async-done | bytes 524304 | tf_op jit(solution)/shard_map/psum | solution.py:9
  275.6 12.9 %convolution_subtract_fusion.3 = f32[2048,1024]{1,0:T(8,128)S(1)} fusion(f32[2048,1024]{1,0:T(8,128)} %param.3, f32[64,2048]{1,0:T(8,128)S(1)} %fusion.3, f32[64,2048]{1,0:T(8,128)S(1)} %bitcast.91, f32[64,1024]{1,0:T(8,128)S(1)} %copy-done.6, f32[64,1024]{1,0:T(8,128)} %get-tuple-element.9), kind=kOutput, calls=%fused_computation.3 | convolution fusion | flops 3223715840 | bytes 18350080 | tf_op jit(solution)/shard_map/dot_general | solution.py:56
  291.9 8.9 %fusion.66 = f32[64,2048]{1,0:T(8,128)} fusion(f32[64,1024]{1,0:T(8,128)S(1)} %copy-done.4, f32[2048,1024]{1,0:T(8,128)S(1)} %convolution_subtract_fusion.3), kind=kOutput, calls=%fused_computation.86 | convolution fusion | flops 1610612736 | bytes 9175040 | tf_op jit(solution)/shard_map/dot_general | solution.py:28
  300.8 25.4 %all-gather.2 = f32[1,64,2048]{2,1,0:T(8,128)S(1)} all-gather(f32[1,64,128]{2,1,0:T(8,128)S(1)} %get-tuple-element.14), channel_id=4, replica_groups=mesh['row'=8,'col'=16] {'col'}, dimensions={2}, use_global_device_ids=true | all-gather | bytes 557056 | tf_op jit(solution)/shard_map/all_gather | solution.py:24
  327.0 58.3 %all-reduce.17.cloned.1.call-done = f32[64,2048]{1,0:T(8,128)} async-done(((f32[64,2048]{1,0:T(8,128)}), f32[64,2048]{1,0:T(8,128)}) %all-reduce.17.cloned.1.call-update) | async-done | bytes 524304 | tf_op jit(solution)/shard_map/psum | solution.py:35
  387.5 24.4 %psum.118 = f32[64,64]{0,1:T(8,128)S(1)} all-reduce(f32[64,64]{0,1:T(8,128)S(1)} %convolution_bitcast_fusion.2), channel_id=1, replica_groups=mesh['row'=8,'col'=16] {'row'}, use_global_device_ids=true, to_apply=%region_6.7 | all-reduce | flops 4096 | bytes 32768 | tf_op jit(solution)/shard_map/psum | solution.py:46
  413.8 57.1 %all-reduce.27.cloned.1.call-done = (f32[64,1024]{1,0:T(8,128)}, f32[64,1024]{1,0:T(8,128)}) async-done(((f32[64,1024]{1,0:T(8,128)}, f32[64,1024]{1,0:T(8,128)}), (f32[64,1024]{1,0:T(8,128)}, f32[64,1024]{1,0:T(8,128)})) %all-reduce.27.cloned.1.call-update) | async-done | bytes 524304 | tf_op jit(solution)/shard_map/psum | solution.py:9
  471.0 12.9 %convolution_subtract_fusion.2 = f32[2048,1024]{1,0:T(8,128)S(1)} fusion(f32[2048,1024]{1,0:T(8,128)} %copy-done.1, f32[64,2048]{1,0:T(8,128)S(1)} %fusion.2, f32[64,2048]{1,0:T(8,128)S(1)} %bitcast.89, f32[64,1024]{1,0:T(8,128)S(1)} %copy-done.4, f32[64,1024]{1,0:T(8,128)} %get-tuple-element.7), kind=kOutput, calls=%fused_computation.2 | convolution fusion | flops 3223715840 | bytes 18350080 | tf_op jit(solution)/shard_map/dot_general | solution.py:56
  496.2 25.4 %all-gather.3 = f32[1,64,2048]{2,1,0:T(8,128)S(1)} all-gather(f32[1,64,128]{2,1,0:T(8,128)S(1)} %get-tuple-element.11), channel_id=5, replica_groups=mesh['row'=8,'col'=16] {'col'}, dimensions={2}, use_global_device_ids=true | all-gather | bytes 557056 | tf_op jit(solution)/shard_map/all_gather | solution.py:24
  522.4 58.3 %all-reduce.19.cloned.1.call-done = f32[64,2048]{1,0:T(8,128)} async-done(((f32[64,2048]{1,0:T(8,128)}), f32[64,2048]{1,0:T(8,128)}) %all-reduce.19.cloned.1.call-update) | async-done | bytes 524304 | tf_op jit(solution)/shard_map/psum | solution.py:35
  582.9 24.4 %psum.122 = f32[64,64]{0,1:T(8,128)S(1)} all-reduce(f32[64,64]{0,1:T(8,128)S(1)} %convolution_bitcast_fusion.1), channel_id=1, replica_groups=mesh['row'=8,'col'=16] {'row'}, use_global_device_ids=true, to_apply=%region_10.11 | all-reduce | flops 4096 | bytes 32768 | tf_op jit(solution)/shard_map/psum | solution.py:46
  609.0 57.3 %all-reduce.25.cloned.1.call-done = (f32[64,1024]{1,0:T(8,128)}, f32[64,1024]{1,0:T(8,128)}) async-done(((f32[64,1024]{1,0:T(8,128)}, f32[64,1024]{1,0:T(8,128)}), (f32[64,1024]{1,0:T(8,128)}, f32[64,1024]{1,0:T(8,128)})) %all-reduce.25.cloned.1.call-update) | async-done | bytes 524304 | tf_op jit(solution)/shard_map/psum | solution.py:9
  666.3 12.9 %convolution_subtract_fusion.1 = f32[2048,1024]{1,0:T(8,128)S(1)} fusion(f32[2048,1024]{1,0:T(8,128)} %copy-done, f32[64,2048]{1,0:T(8,128)S(1)} %fusion.1, f32[64,2048]{1,0:T(8,128)S(1)} %bitcast.88, f32[64,1024]{1,0:T(8,128)S(1)} %copy-done.3, f32[64,1024]{1,0:T(8,128)} %get-tuple-element.5), kind=kOutput, calls=%fused_computation.1 | convolution fusion | flops 3223715840 | bytes 18350080 | tf_op jit(solution)/shard_map/dot_general | solution.py:56
  682.6 8.9 %fusion.68 = f32[64,2048]{1,0:T(8,128)} fusion(f32[64,1024]{1,0:T(8,128)S(1)} %copy-done.5, f32[2048,1024]{1,0:T(8,128)S(1)} %convolution_subtract_fusion.1), kind=kOutput, calls=%fused_computation.88 | convolution fusion | flops 1610612736 | bytes 9175040 | tf_op jit(solution)/shard_map/dot_general | solution.py:28
  691.6 84.2 %all-reduce.21.cloned.1.call-done = f32[64,2048]{1,0:T(8,128)} async-done(((f32[64,2048]{1,0:T(8,128)}), f32[64,2048]{1,0:T(8,128)}) %all-reduce.21.cloned.1.call-update) | async-done | bytes 524304 | tf_op jit(solution)/shard_map/psum | solution.py:35
  778.1 24.8 %psum.126 = f32[64,64]{0,1:T(8,128)S(1)} all-reduce(f32[64,64]{0,1:T(8,128)S(1)} %convolution_bitcast_fusion), channel_id=1, replica_groups=mesh['row'=8,'col'=16] {'row'}, use_global_device_ids=true, to_apply=%region_14.15 | all-reduce | flops 4096 | bytes 32768 | tf_op jit(solution)/shard_map/psum | solution.py:46
  804.3 56.4 %all-reduce.23.cloned.1.call-done = f32[64,1024]{1,0:T(8,128)} async-done(((f32[64,1024]{1,0:T(8,128)}), f32[64,1024]{1,0:T(8,128)}) %all-reduce.23.cloned.1.call-update) | async-done | bytes 262160 | tf_op jit(solution)/shard_map/psum | solution.py:9
  860.7 11.2 %convolution_subtract_fusion = f32[2048,1024]{1,0:T(8,128)} fusion(f32[2048,1024]{1,0:T(8,128)} %copy-done.2, f32[64,2048]{1,0:T(8,128)S(1)} %fusion, f32[64,2048]{1,0:T(8,128)S(1)} %bitcast.90, f32[64,1024]{1,0:T(8,128)S(1)} %copy-done.5, f32[64,1024]{1,0:T(8,128)} %all-reduce.23.cloned.1.call-done), kind=kOutput, calls=%fused_computation | convolution fusion | flops 3223715840 | bytes 18350080 | tf_op jit(solution)/shard_map/dot_general | solution.py:56
  (60 shorter events, 38.8 us)
Async XLA Ops:
  6.5 183.3 %copy-start.7 = (f32[4,64,64]{2,1,0:T(8,128)S(1)}, f32[4,64,64]{2,1,0:T(8,128)}, u32[]{:S(2)}) copy-start(f32[4,64,64]{2,1,0:T(8,128)} %param.5) | copy-start | bytes 196612
  6.5 86.9 %all-reduce.13.cloned.1.call-start = ((), (), s32[]{:S(2)}) async-start(), calls=%async_computation | async-start | bytes 524288 | tf_op jit(solution)/shard_map/psum | solution.py:9
  33.4 156.5 %all-reduce.15.cloned.1.call-start = ((), (), s32[]{:S(2)}) async-start(), calls=%async_computation.1 | async-start | bytes 1048576 | tf_op jit(solution)/shard_map/psum | solution.py:35
  93.4 182.2 %copy-start.6 = (f32[64,1024]{1,0:T(8,128)S(1)}, f32[64,1024]{1,0:T(8,128)}, u32[]{:S(2)}) copy-start(f32[64,1024]{1,0:T(8,128)} %all-reduce.13.cloned.1.call-done) | copy-start | bytes 786436
  105.7 169.9 %all-reduce.29.cloned.1.call-start = ((), (), s32[]{:S(2)}) async-start(), calls=%async_computation.8 | async-start | bytes 1048576 | tf_op jit(solution)/shard_map/psum | solution.py:9
  218.1 167.2 %all-reduce.17.cloned.1.call-start = ((), (), s32[]{:S(2)}) async-start(), calls=%async_computation.2 | async-start | bytes 1048576 | tf_op jit(solution)/shard_map/psum | solution.py:35
  275.6 16.3 %copy-start.4 = (f32[64,1024]{1,0:T(8,128)S(1)}, f32[64,1024]{1,0:T(8,128)}, u32[]{:S(2)}) copy-start(f32[64,1024]{1,0:T(8,128)} %get-tuple-element.10) | copy-start | bytes 786436
  288.4 3.4 copy-start.1
  300.8 170.2 %all-reduce.27.cloned.1.call-start = ((), (), s32[]{:S(2)}) async-start(), calls=%async_computation.7 | async-start | bytes 1048576 | tf_op jit(solution)/shard_map/psum | solution.py:9
  413.4 167.3 %all-reduce.19.cloned.1.call-start = ((), (), s32[]{:S(2)}) async-start(), calls=%async_computation.3 | async-start | bytes 1048576 | tf_op jit(solution)/shard_map/psum | solution.py:35
  471.0 16.3 %copy-start.3 = (f32[64,1024]{1,0:T(8,128)S(1)}, f32[64,1024]{1,0:T(8,128)}, u32[]{:S(2)}) copy-start(f32[64,1024]{1,0:T(8,128)} %get-tuple-element.8) | copy-start | bytes 786436
  483.9 3.4 copy-start
  496.2 170.1 %all-reduce.25.cloned.1.call-start = ((), (), s32[]{:S(2)}) async-start(), calls=%async_computation.6 | async-start | bytes 1048576 | tf_op jit(solution)/shard_map/psum | solution.py:9
  608.8 167.0 %all-reduce.21.cloned.1.call-start = ((), (), s32[]{:S(2)}) async-start(), calls=%async_computation.4 | async-start | bytes 1048576 | tf_op jit(solution)/shard_map/psum | solution.py:35
  666.3 16.3 %copy-start.5 = (f32[64,1024]{1,0:T(8,128)S(1)}, f32[64,1024]{1,0:T(8,128)}, u32[]{:S(2)}) copy-start(f32[64,1024]{1,0:T(8,128)} %get-tuple-element.6) | copy-start | bytes 786436
  679.2 3.4 copy-start.2
  691.5 169.2 %all-reduce.23.cloned.1.call-start = ((), (), s32[]{:S(2)}) async-start(), calls=%async_computation.5 | async-start | bytes 524288 | tf_op jit(solution)/shard_map/psum | solution.py:9
Sparse Core Ops, SparseCore 0:
  33.5 59.8 all-reduce.12
  105.8 84.0 all-reduce.14
  218.2 57.3 all-reduce.28
  300.9 84.2 all-reduce.16
  413.5 57.4 all-reduce.26
  496.3 84.2 all-reduce.18
  608.9 57.3 all-reduce.24
  691.6 84.1 all-reduce.20
  804.4 56.2 all-reduce.22
where the time goes:
time: 886 us; the launch traced here: 879 us
  waiting for transfers between devices  547 us (62%)
  blocking collectives  199 us (22%)
  matrix products  101 us (11%)
  between operations  13.6 us (2%)
  local copies, waits for them, and re-layouts  11 us (1%)
    psum x5, waiting for transfers between devices, broadcast(): return lax.psum(kept, axis)  288 us
    psum x4, waiting for transfers between devices, shards(): product_rows = lax.psum(partial_value, 'col')  259 us
    all_gather x4, blocking collectives, shards(): reflect_rows = lax.all_gather(piece, 'col', axis=1, tiled=True)  101 us
    psum x4, blocking collectives, shards(): inner = lax.psum(local_inner, 'row')  98.1 us
    dot_general x4, matrix products, shards(): lax.dot_general(left_block, right_block, (((0,), (0,)), ((), ())), precis...  49.8 us
    dot_general x4, matrix products, shards(): lax.dot_general(reflect_cols, matrix, (((1,), (1,)), ((), ())), precision...  39 us
  transfers between devices with their start and end apart: 9, of which 9 were waited for; matrix products, arithmetic and copies ran while one was open for 0% of the time, Pallas kernels for 0%

commit v1 on v0

--- a/solution.py
+++ b/solution.py
@@ -6,7 +6,7 @@
 
 def broadcast(value, axis, source):
     kept = jnp.where(lax.axis_index(axis) == source, value, 0).astype(value.dtype)
-    return lax.psum(kept, axis)
+    return jnp.sum(lax.all_gather(kept, axis), axis=0)
 
 
 def shards(symmetric, reflectors, tri_factor):

time: 886 us -> 724 us (0.82)
  waiting for transfers between devices: 547 us -> 380 us
  other arithmetic: 5.77 us -> 19.8 us
  matrix products: 101 us -> 89.6 us
    psum x5 -> x0, waiting for transfers between devices: 288 us -> none  [broadcast(): return lax.psum(kept, axis)]
    all_gather x0 -> x8, waiting for transfers between devices: none -> 117 us  [broadcast(): return jnp.sum(lax.all_gather(kept, axis), axis=0)]
    reduce_sum x0 -> x8, other arithmetic: none -> 14 us  [broadcast(): return jnp.sum(lax.all_gather(kept, axis), axis=0)]
    dot_general x4, matrix products: 49.8 us -> 39.9 us  [shards(): lax.dot_general(left_block, right_block, (((0,), (0,)), ((), ())), precis...]
  transfers between devices with their start and end apart: 9 -> 12, of which waited for: 9 -> 9; matrix products, arithmetic and copies ran while one was open for 0% -> 3% of each run, Pallas kernels for 0% -> 0%
where the time goes in v1:
time: 724 us; the launch traced here: 717 us
  waiting for transfers between devices  380 us (52%)
  blocking collectives  201 us (28%)
  matrix products  89.6 us (12%)
  other arithmetic  19.8 us (3%)
  between operations  14.1 us (2%)
  local copies, waits for them, and re-layouts  11 us (2%)
    psum x4, waiting for transfers between devices, shards(): product_rows = lax.psum(partial_value, 'col')  263 us
    all_gather x8, waiting for transfers between devices, broadcast(): return jnp.sum(lax.all_gather(kept, axis), axis=0)  117 us
    all_gather x4, blocking collectives, shards(): reflect_rows = lax.all_gather(piece, 'col', axis=1, tiled=True)  102 us
    psum x4, blocking collectives, shards(): inner = lax.psum(local_inner, 'row')  99.2 us
    dot_general x4, matrix products, shards(): lax.dot_general(left_block, right_block, (((0,), (0,)), ((), ())), precis...  39.9 us
    dot_general x4, matrix products, shards(): lax.dot_general(reflect_cols, matrix, (((1,), (1,)), ((), ())), precision...  37.9 us
  transfers between devices with their start and end apart: 12, of which 9 were waited for; matrix products, arithmetic and copies ran while one was open for 3% of the time, Pallas kernels for 0%

profile of v1, /device:TPU:0, one launch (start us, length us, event | category | flops | bytes accessed | tf_op | source)
XLA Modules:
  0.0 717.4 jit_solution(12885770256622975049)
XLA Ops:
  7.4 25.2 %all-gather = f32[1,64,2048]{2,1,0:T(8,128)S(1)} all-gather(f32[1,64,128]{2,1,0:T(8,128)S(1)} %get-tuple-element.7), channel_id=2, replica_groups=mesh['row'=8,'col'=16] {'col'}, dimensions={2}, use_global_device_ids=true | all-gather | bytes 557056 | tf_op jit(solution)/shard_map/all_gather | solution.py:24
  33.4 25.3 %all-gather.33.cloned.1.call-done = f32[1,512,1024]{2,1,0:T(8,128)} async-done(((f32[1,64,1024]{2,1,0:T(8,128)}), f32[1,512,1024]{2,1,0:T(8,128)}) %all-gather.33.cloned.1.call-update) | async-done | bytes 2097168 | tf_op jit(solution)/shard_map/all_gather | solution.py:9
  60.5 11.1 %fusion.65 = f32[64,2048]{1,0:T(8,128)} fusion(f32[64,1024]{1,0:T(8,128)S(1)} %reduce_sum.72, f32[2048,1024]{1,0:T(8,128)} %param.3), kind=kOutput, calls=%fused_computation.85 | convolution fusion | flops 1610612736 | bytes 9175040 | tf_op jit(solution)/shard_map/dot_general | solution.py:28
  71.7 25.6 %all-gather.3 = f32[1,64,2048]{2,1,0:T(8,128)S(1)} all-gather(f32[1,64,128]{2,1,0:T(8,128)S(1)} %get-tuple-element.6), channel_id=5, replica_groups=mesh['row'=8,'col'=16] {'col'}, dimensions={2}, use_global_device_ids=true | all-gather | bytes 557056 | tf_op jit(solution)/shard_map/all_gather | solution.py:24
  98.1 59.3 %all-reduce.5.cloned.1.call-done = f32[64,2048]{1,0:T(8,128)} async-done(((f32[64,2048]{1,0:T(8,128)}), f32[64,2048]{1,0:T(8,128)}) %all-reduce.5.cloned.1.call-update) | async-done | bytes 524304 | tf_op jit(solution)/shard_map/psum | solution.py:35
  159.6 24.8 %psum.57 = f32[64,64]{0,1:T(8,128)S(1)} all-reduce(f32[64,64]{0,1:T(8,128)S(1)} %convolution_bitcast_fusion.3), channel_id=1, replica_groups=mesh['row'=8,'col'=16] {'row'}, use_global_device_ids=true, to_apply=%region_2.3 | all-reduce | flops 4096 | bytes 32768 | tf_op jit(solution)/shard_map/psum | solution.py:46
  188.2 23.2 %all-gather.25.cloned.1.call-done = f32[512,1024]{1,0:T(8,128)} async-done(((f32[64,1024]{1,0:T(8,128)}), f32[512,1024]{1,0:T(8,128)}) %all-gather.25.cloned.1.call-update) | async-done | bytes 2097168 | tf_op jit(solution)/shard_map/all_gather | solution.py:9
  213.2 9.6 %convolution_subtract_fusion.3 = f32[2048,1024]{1,0:T(8,128)S(1)} fusion(f32[2048,1024]{1,0:T(8,128)} %param.3, f32[64,2048]{1,0:T(8,128)S(1)} %fusion.3, f32[64,2048]{1,0:T(8,128)S(1)} %bitcast.91, f32[64,1024]{1,0:T(8,128)S(1)} %reduce_sum.72, f32[64,1024]{1,0:T(8,128)S(1)} %reduce_sum.73), kind=kOutput, calls=%fused_computation.3 | convolution fusion | flops 3223715840 | bytes 18350080 | tf_op jit(solution)/shard_map/dot_general | solution.py:56
  226.2 8.9 %fusion.66 = f32[64,2048]{1,0:T(8,128)} fusion(f32[64,1024]{1,0:T(8,128)S(1)} %reduce_sum.74, f32[2048,1024]{1,0:T(8,128)S(1)} %convolution_subtract_fusion.3), kind=kOutput, calls=%fused_computation.86 | convolution fusion | flops 1610612736 | bytes 9175040 | tf_op jit(solution)/shard_map/dot_general | solution.py:28
  235.2 25.6 %all-gather.6 = f32[1,64,2048]{2,1,0:T(8,128)S(1)} all-gather(f32[1,64,128]{2,1,0:T(8,128)S(1)} %get-tuple-element.8), channel_id=8, replica_groups=mesh['row'=8,'col'=16] {'col'}, dimensions={2}, use_global_device_ids=true | all-gather | bytes 557056 | tf_op jit(solution)/shard_map/all_gather | solution.py:24
  261.6 59.2 %all-reduce.7.cloned.1.call-done = f32[64,2048]{1,0:T(8,128)} async-done(((f32[64,2048]{1,0:T(8,128)}), f32[64,2048]{1,0:T(8,128)}) %all-reduce.7.cloned.1.call-update) | async-done | bytes 524304 | tf_op jit(solution)/shard_map/psum | solution.py:35
  323.1 25.3 %psum.59 = f32[64,64]{0,1:T(8,128)S(1)} all-reduce(f32[64,64]{0,1:T(8,128)S(1)} %convolution_bitcast_fusion.2), channel_id=1, replica_groups=mesh['row'=8,'col'=16] {'row'}, use_global_device_ids=true, to_apply=%region_6.7 | all-reduce | flops 4096 | bytes 32768 | tf_op jit(solution)/shard_map/psum | solution.py:46
  351.7 23.0 %all-gather.27.cloned.1.call-done = f32[512,1024]{1,0:T(8,128)} async-done(((f32[64,1024]{1,0:T(8,128)}), f32[512,1024]{1,0:T(8,128)}) %all-gather.27.cloned.1.call-update) | async-done | bytes 2097168 | tf_op jit(solution)/shard_map/all_gather | solution.py:9
  376.4 9.6 %convolution_subtract_fusion.2 = f32[2048,1024]{1,0:T(8,128)S(1)} fusion(f32[2048,1024]{1,0:T(8,128)} %copy-done.1, f32[64,2048]{1,0:T(8,128)S(1)} %fusion.2, f32[64,2048]{1,0:T(8,128)S(1)} %bitcast.89, f32[64,1024]{1,0:T(8,128)S(1)} %reduce_sum.74, f32[64,1024]{1,0:T(8,128)S(1)} %reduce_sum.75), kind=kOutput, calls=%fused_computation.2 | convolution fusion | flops 3223715840 | bytes 18350080 | tf_op jit(solution)/shard_map/dot_general | solution.py:56
  389.3 8.9 %fusion.67 = f32[64,2048]{1,0:T(8,128)} fusion(f32[64,1024]{1,0:T(8,128)S(1)} %reduce_sum.76, f32[2048,1024]{1,0:T(8,128)S(1)} %convolution_subtract_fusion.2), kind=kOutput, calls=%fused_computation.87 | convolution fusion | flops 1610612736 | bytes 9175040 | tf_op jit(solution)/shard_map/dot_general | solution.py:28
  398.3 25.6 %all-gather.9 = f32[1,64,2048]{2,1,0:T(8,128)S(1)} all-gather(f32[1,64,128]{2,1,0:T(8,128)S(1)} %get-tuple-element.5), channel_id=11, replica_groups=mesh['row'=8,'col'=16] {'col'}, dimensions={2}, use_global_device_ids=true | all-gather | bytes 557056 | tf_op jit(solution)/shard_map/all_gather | solution.py:24
  425.0 59.1 %all-reduce.9.cloned.1.call-done = f32[64,2048]{1,0:T(8,128)} async-done(((f32[64,2048]{1,0:T(8,128)}), f32[64,2048]{1,0:T(8,128)}) %all-reduce.9.cloned.1.call-update) | async-done | bytes 524304 | tf_op jit(solution)/shard_map/psum | solution.py:35
  486.3 24.8 %psum.61 = f32[64,64]{0,1:T(8,128)S(1)} all-reduce(f32[64,64]{0,1:T(8,128)S(1)} %convolution_bitcast_fusion.1), channel_id=1, replica_groups=mesh['row'=8,'col'=16] {'row'}, use_global_device_ids=true, to_apply=%region_10.11 | all-reduce | flops 4096 | bytes 32768 | tf_op jit(solution)/shard_map/psum | solution.py:46
  514.4 23.7 %all-gather.29.cloned.1.call-done = f32[512,1024]{1,0:T(8,128)} async-done(((f32[64,1024]{1,0:T(8,128)}), f32[512,1024]{1,0:T(8,128)}) %all-gather.29.cloned.1.call-update) | async-done | bytes 2097168 | tf_op jit(solution)/shard_map/all_gather | solution.py:9
  539.8 9.6 %convolution_subtract_fusion.1 = f32[2048,1024]{1,0:T(8,128)S(1)} fusion(f32[2048,1024]{1,0:T(8,128)} %copy-done, f32[64,2048]{1,0:T(8,128)S(1)} %fusion.1, f32[64,2048]{1,0:T(8,128)S(1)} %bitcast.88, f32[64,1024]{1,0:T(8,128)S(1)} %reduce_sum.76, f32[64,1024]{1,0:T(8,128)S(1)} %reduce_sum.77), kind=kOutput, calls=%fused_computation.1 | convolution fusion | flops 3223715840 | bytes 18350080 | tf_op jit(solution)/shard_map/dot_general | solution.py:56
  562.1 85.3 %all-reduce.11.cloned.1.call-done = f32[64,2048]{1,0:T(8,128)} async-done(((f32[64,2048]{1,0:T(8,128)}), f32[64,2048]{1,0:T(8,128)}) %all-reduce.11.cloned.1.call-update) | async-done | bytes 524304 | tf_op jit(solution)/shard_map/psum | solution.py:35
  649.6 24.4 %psum.63 = f32[64,64]{0,1:T(8,128)S(1)} all-reduce(f32[64,64]{0,1:T(8,128)S(1)} %convolution_bitcast_fusion), channel_id=1, replica_groups=mesh['row'=8,'col'=16] {'row'}, use_global_device_ids=true, to_apply=%region_14.15 | all-reduce | flops 4096 | bytes 32768 | tf_op jit(solution)/shard_map/psum | solution.py:46
  675.6 21.8 %all-gather.31.cloned.1.call-done = f32[512,1024]{1,0:T(8,128)} async-done(((f32[64,1024]{1,0:T(8,128)}), f32[512,1024]{1,0:T(8,128)}) %all-gather.31.cloned.1.call-update) | async-done | bytes 2097168 | tf_op jit(solution)/shard_map/all_gather | solution.py:9
  699.1 11.2 %convolution_subtract_fusion = f32[2048,1024]{1,0:T(8,128)} fusion(f32[2048,1024]{1,0:T(8,128)} %copy-done.2, f32[64,2048]{1,0:T(8,128)S(1)} %fusion, f32[64,2048]{1,0:T(8,128)S(1)} %bitcast.90, f32[64,1024]{1,0:T(8,128)S(1)} %reduce_sum.78, f32[64,1024]{1,0:T(8,128)S(1)} %reduce_sum.79), kind=kOutput, calls=%fused_computation | convolution fusion | flops 3223715840 | bytes 18350080 | tf_op jit(solution)/shard_map/dot_general | solution.py:56
  (69 shorter events, 53.2 us)
Async XLA Ops:
  6.5 150.9 %copy-start.3 = (f32[4,64,64]{2,1,0:T(8,128)S(1)}, f32[4,64,64]{2,1,0:T(8,128)}, u32[]{:S(2)}) copy-start(f32[4,64,64]{2,1,0:T(8,128)} %param.5) | copy-start | bytes 196612
  6.5 52.2 %all-gather.33.cloned.1.call-start = ((), (), s32[]{:S(2)}) async-start(), calls=%async_computation.8 | async-start | bytes 2359296 | tf_op jit(solution)/shard_map/all_gather | solution.py:9
  33.4 124.0 %all-reduce.5.cloned.1.call-start = ((), (), s32[]{:S(2)}) async-start(), calls=%async_computation | async-start | bytes 1048576 | tf_op jit(solution)/shard_map/psum | solution.py:35
  71.6 114.9 %all-gather.35.cloned.1.call-start = ((), (), s32[]{:S(2)}) async-start(), calls=%async_computation.9 | async-start | bytes 2359296 | tf_op jit(solution)/shard_map/all_gather | solution.py:9
  98.0 113.4 %all-gather.25.cloned.1.call-start = ((), (), s32[]{:S(2)}) async-start(), calls=%async_computation.4 | async-start | bytes 2359296 | tf_op jit(solution)/shard_map/all_gather | solution.py:9
  185.9 134.9 %all-reduce.7.cloned.1.call-start = ((), (), s32[]{:S(2)}) async-start(), calls=%async_computation.1 | async-start | bytes 1048576 | tf_op jit(solution)/shard_map/psum | solution.py:35
  222.8 3.4 copy-start.1
  235.1 114.8 %all-gather.37.cloned.1.call-start = ((), (), s32[]{:S(2)}) async-start(), calls=%async_computation.10 | async-start | bytes 2359296 | tf_op jit(solution)/shard_map/all_gather | solution.py:9
  261.5 113.1 %all-gather.27.cloned.1.call-start = ((), (), s32[]{:S(2)}) async-start(), calls=%async_computation.5 | async-start | bytes 2359296 | tf_op jit(solution)/shard_map/all_gather | solution.py:9
  349.8 134.2 %all-reduce.9.cloned.1.call-start = ((), (), s32[]{:S(2)}) async-start(), calls=%async_computation.2 | async-start | bytes 1048576 | tf_op jit(solution)/shard_map/psum | solution.py:35
  385.9 3.4 copy-start
  398.3 114.3 %all-gather.39.cloned.1.call-start = ((), (), s32[]{:S(2)}) async-start(), calls=%async_computation.11 | async-start | bytes 2359296 | tf_op jit(solution)/shard_map/all_gather | solution.py:9
  424.7 113.4 %all-gather.29.cloned.1.call-start = ((), (), s32[]{:S(2)}) async-start(), calls=%async_computation.6 | async-start | bytes 2359296 | tf_op jit(solution)/shard_map/all_gather | solution.py:9
  512.5 134.8 %all-reduce.11.cloned.1.call-start = ((), (), s32[]{:S(2)}) async-start(), calls=%async_computation.3 | async-start | bytes 1048576 | tf_op jit(solution)/shard_map/psum | solution.py:35
  549.4 3.4 copy-start.2
  561.8 135.6 %all-gather.31.cloned.1.call-start = ((), (), s32[]{:S(2)}) async-start(), calls=%async_computation.7 | async-start | bytes 2359296 | tf_op jit(solution)/shard_map/all_gather | solution.py:9
Sparse Core Ops, SparseCore 0:
  33.5 25.1 all-gather.32
  71.7 85.6 all-reduce.4
  159.2 24.7 all-gather.34
  186.0 25.3 all-gather.24
  235.2 85.5 all-reduce.6
  322.4 24.7 all-gather.36
  349.9 24.6 all-gather.26
  398.4 85.5 all-reduce.8
  485.9 24.7 all-gather.38
  512.7 25.3 all-gather.28
  561.9 85.4 all-reduce.10
  675.7 21.6 all-gather.30
